TPU v7x, 512 devices: a whole 4x4x16 slice. The times are simulated.
512 devices in a mesh: guide: 2 (over core), dp: 16 (over y, x), mp: 16 (over z).
Axes of the slice: x: 4, y: 4, z: 16, core: 2. Of those that a mesh axis runs over, the one named last changes fastest.
Arguments:
- states: bfloat16 [2, 128, 2048], P('guide', 'dp'), may hold values from -6 to 6
- lengths: int32 [2, 128], P('guide', 'dp'), may hold values from 1 to 32768, as said below
- sink_cache: bfloat16 [2, 128, 16, 2, 4, 128], P('guide', 'dp', 'mp'), may hold values from -48 to 48
- window_cache: bfloat16 [2, 128, 16, 2, 256, 128], P('guide', 'dp', 'mp'), may hold values from -360 to 360
- qkv_weight: bfloat16 [2048, 3, 16, 128], P(None, None, 'mp'), may hold values from -0.125 to 0.125
- out_weight: bfloat16 [16, 128, 2048], P('mp'), may hold values from -0.125 to 0.125
- expert_ids: int32 [2, 128, 8], replicated, may hold values from 0 to 63, all different within a row; in each aligned block of 8 rows (0 to 7, 8 to 15, ..., all dimensions but the last counted through in order) at most 2 rows name the same one
- route_weight: float32 [2, 128, 8], replicated, may hold values from 0.5 to 2
- expert_in: bfloat16 [2, 2048, 65536], P(None, None, ('guide', 'dp', 'mp')), may hold values from -0.125 to 0.125
- expert_out: bfloat16 [65536, 2048], P(('guide', 'dp', 'mp')), may hold values from -0.1875 to 0.1875
- vocab_weight: bfloat16 [2048, 26624], P(('guide', 'dp'), 'mp'), may hold values from -0.125 to 0.125
- guidance: float32 [128], P('dp'), may hold values from 1 to 5
Outputs:
- guided: float32 [128, 16, 2, 832], P('dp', 'mp', 'guide')
Inputs may be any that keep to these rules, and one draw needn't show every extreme that they name: `lengths`: one stream of one request has exactly 32768 cached positions. `expert_ids`: taking the tokens streams first, then requests, in aligned blocks of 8 tokens (the tokens of one device), no expert is named by more than 2 tokens of a block, a bound that some block reaches.
All inputs are finite; a program needn't handle non-finite values.
Results may differ from a plain program's by a relative error of at most 0.025.
Values may be sent and summed in bfloat16 or wider, within the bound.
A program may use at most 64 MiB of HBM per device.

v0:
```python
import math
import jax
import jax.numpy as jnp
from jax import lax
from jax.sharding import PartitionSpec as P

FFE = 1024
EPSILON = 1e-05


def partner(block, axis, stride):
    count = lax.axis_size(axis)
    route = []
    for low in range(count):
        high = low | 1 << stride
        if high != low and high < count:
            route += [(low, high), (high, low)]
    return lax.ppermute(block, axis, route)


def rms_norm(values):
    return values * lax.rsqrt(jnp.mean(values * values, axis=-1, keepdims=True) + EPSILON)


def rotate(vectors, positions):
    full_width = vectors.shape[-1]
    half_width = full_width // 2
    step_index = jnp.arange(half_width, dtype=jnp.float32)
    inverse = jnp.exp(step_index * (-2.0 * math.log(10000.0) / full_width))
    angles = positions.astype(jnp.float32)[:, None] * inverse[None, :]
    cosine = jnp.cos(angles)[:, None, :]
    sine_part = jnp.sin(angles)[:, None, :]
    first_half = vectors[..., :half_width]
    second = vectors[..., half_width:]
    return jnp.concatenate(
        [first_half * cosine - second * sine_part, second * cosine + first_half * sine_part],
        axis=-1,
    )


def body(
    states,
    lengths,
    sink_cache,
    window_cache,
    qkv_weight,
    out_weight,
    expert_ids,
    route_weight,
    expert_in,
    expert_out,
    vocab_weight,
    guidance,
):
    hidden = states[0]
    own_lengths = lengths[0]
    request_count = hidden.shape[0]
    normed = rms_norm(hidden.astype(jnp.float32)).astype(jnp.bfloat16)
    projected = jnp.einsum("rd,dthe->rthe", normed, qkv_weight, preferred_element_type=jnp.float32)
    query_rot = rotate(projected[:, 0], own_lengths).astype(jnp.bfloat16)
    fresh_key = rotate(projected[:, 1], own_lengths).astype(jnp.bfloat16)
    fresh_value = projected[:, 2].astype(jnp.bfloat16)
    sink_rows = sink_cache[0]
    window_rows = window_cache[0]
    sink_count = sink_rows.shape[3]
    window_count = window_rows.shape[3]
    root_size = math.sqrt(query_rot.shape[-1])
    sink_scores = (
        jnp.einsum(
            "rhe,rhse->rhs", query_rot, sink_rows[:, :, 0], preferred_element_type=jnp.float32
        )
        / root_size
    )
    window_scores = (
        jnp.einsum(
            "rhe,rhwe->rhw", query_rot, window_rows[:, :, 0], preferred_element_type=jnp.float32
        )
        / root_size
    )
    self_scores = (
        jnp.einsum("rhe,rhe->rh", query_rot, fresh_key, preferred_element_type=jnp.float32)
        / root_size
    )
    length_limit = own_lengths[:, None, None]
    sink_valid = jnp.arange(sink_count, dtype=jnp.int32)[None, None, :] < length_limit
    window_valid = (
        jnp.arange(window_count, dtype=jnp.int32)[None, None, :]
        >= sink_count + window_count - length_limit
    )
    sink_scores = jnp.where(sink_valid, sink_scores, -1e30)
    window_scores = jnp.where(window_valid, window_scores, -1e30)
    highest = jnp.maximum(
        jnp.maximum(jnp.max(sink_scores, axis=-1), jnp.max(window_scores, axis=-1)), self_scores
    )
    sink_exp = jnp.exp(sink_scores - highest[..., None])
    window_exp = jnp.exp(window_scores - highest[..., None])
    self_exp = jnp.exp(self_scores - highest)
    totals = jnp.sum(sink_exp, axis=-1) + jnp.sum(window_exp, axis=-1) + self_exp
    sink_prob = (sink_exp / totals[..., None]).astype(jnp.bfloat16)
    window_prob = (window_exp / totals[..., None]).astype(jnp.bfloat16)
    self_prob = (self_exp / totals).astype(jnp.bfloat16)
    mixture = (
        jnp.einsum(
            "rhs,rhse->rhe", sink_prob, sink_rows[:, :, 1], preferred_element_type=jnp.float32
        )
        + jnp.einsum(
            "rhw,rhwe->rhe", window_prob, window_rows[:, :, 1], preferred_element_type=jnp.float32
        )
        + self_prob[..., None].astype(jnp.float32) * fresh_value.astype(jnp.float32)
    ).astype(jnp.bfloat16)
    partial_out = jnp.einsum("rhe,hed->rd", mixture, out_weight, preferred_element_type=jnp.float32)
    attention_out = lax.psum(partial_out, "mp")
    residual = (hidden.astype(jnp.float32) + attention_out).astype(jnp.bfloat16)
    moe_in = rms_norm(residual.astype(jnp.float32)).astype(jnp.bfloat16)
    unit_count = expert_in.shape[2]
    unit_start = lax.axis_index(("guide", "dp", "mp")) * unit_count
    unit_expert = (unit_start + jnp.arange(unit_count, dtype=jnp.int32)) // FFE
    choice_rows = expert_ids.reshape(-1, expert_ids.shape[-1])
    route_rows = route_weight.reshape(-1, route_weight.shape[-1])
    coefficient = jnp.sum(
        jnp.where(
            choice_rows[:, :, None] == unit_expert[None, None, :], route_rows[:, :, None], 0.0
        ),
        axis=1,
    )
    piece = lax.all_gather(moe_in, ("guide", "dp"), axis=0, tiled=True)
    gate = jnp.dot(piece, expert_in[0], preferred_element_type=jnp.float32)
    upward = jnp.dot(piece, expert_in[1], preferred_element_type=jnp.float32)
    activated = (jax.nn.silu(gate) * upward * coefficient).astype(jnp.bfloat16)
    expert_terms = jnp.dot(activated, expert_out, preferred_element_type=jnp.float32)
    expert_part = lax.psum_scatter(expert_terms, ("guide", "dp"), scatter_dimension=0, tiled=True)
    expert_total = lax.psum(expert_part, "mp")
    final = rms_norm(residual.astype(jnp.float32) + expert_total).astype(jnp.bfloat16)
    final_all = lax.all_gather(final, ("guide", "dp"), axis=0, tiled=True)
    row_share = vocab_weight.shape[0]
    share_start = lax.axis_index(("guide", "dp")) * row_share
    final_cols = lax.dynamic_slice_in_dim(final_all, share_start, row_share, 1)
    logits = lax.psum_scatter(
        jnp.dot(final_cols, vocab_weight, preferred_element_type=jnp.float32).astype(jnp.bfloat16),
        ("guide", "dp"),
        scatter_dimension=0,
        tiled=True,
    ).astype(jnp.float32)
    half_width = logits.shape[1] // 2
    stream_index = lax.axis_index("guide")
    own_half = lax.dynamic_slice_in_dim(logits, stream_index * half_width, half_width, 1)
    other_half = lax.dynamic_slice_in_dim(logits, (1 - stream_index) * half_width, half_width, 1)
    partner_logits = partner(other_half, "guide", 0)
    is_conditional = stream_index == 0
    conditional = jnp.where(is_conditional, own_half, partner_logits)
    unconditional = jnp.where(is_conditional, partner_logits, own_half)
    guided = unconditional + guidance[:, None] * (conditional - unconditional)
    return guided.reshape(request_count, 1, 1, half_width)


def solution(mesh):
    in_specs = (
        P("guide", "dp", None),
        P("guide", "dp"),
        P("guide", "dp", "mp", None, None, None),
        P("guide", "dp", "mp", None, None, None),
        P(None, None, "mp", None),
        P("mp", None, None),
        P(),
        P(),
        P(None, None, ("guide", "dp", "mp")),
        P(("guide", "dp", "mp"), None),
        P(("guide", "dp"), "mp"),
        P("dp"),
    )
    out_specs = P("dp", "mp", "guide", None)
    return jax.shard_map(body, mesh=mesh, in_specs=in_specs, out_specs=out_specs, check_vma=False)
```

profile of v0, /device:TPU:1, one launch (start us, length us, event | category | flops | bytes accessed | tf_op | source)
XLA Modules:
  0.0 657.1 jit_solution(2036525778644055514)
XLA Ops:
  6.5 0.0 all-reduce.5.cloned.1.call-start
  6.6 0.8 bitcast_convert_fusion
  7.4 0.8 broadcast_subtract_fusion
  8.2 0.9 fusion.23
  9.1 1.2 fusion
  10.3 0.1 fusion.67
  10.4 0.1 fusion.73
  10.5 0.2 fusion.6
  10.7 0.1 fusion.35
  10.9 0.1 copy.28
  10.9 0.2 fusion.57
  11.1 0.2 fusion.46
  11.4 0.2 fusion.37
  11.6 0.1 fusion.58
  11.7 0.2 fusion.5
  11.9 0.1 copy.33
  12.0 0.1 fusion.36
  12.1 0.9 fusion.11
  13.0 0.0 all-reduce.5.cloned.1.call-update
  13.0 0.0 all-gather.3.cloned.1.call-start
  13.0 128.0 %all-reduce.5.cloned.1.call-done = f32[8,2048]{1,0:T(8,128)} async-done(((f32[8,2048]{1,0:T(8,128)}), f32[8,2048]{1,0:T(8,128)}) %all-reduce.5.cloned.1.call-update) | async-done | bytes 65552 | tf_op jit(solution)/shard_map/psum | solution.py:112
  141.0 1.0 fusion.26
  142.0 0.7 fusion.27
  142.7 0.0 all-gather.3.cloned.1.call-update
  142.7 0.0 reduce-scatter.2.cloned.1.call-start
  142.8 0.1 copy.24
  142.9 0.1 copy.25
  143.1 1.3 select_reduce_fusion
  144.4 65.6 %all-gather.3.cloned.1.call-done = bf16[256,2048]{1,0:T(8,128)(2,1)} async-done(((bf16[8,2048]{1,0:T(8,128)(2,1)}), bf16[256,2048]{1,0:T(8,128)(2,1)}) %all-gather.3.cloned.1.call-update) | async-done | bytes 1048592 | tf_op jit(solution)/shard_map/all_gather | solution.py:126
  210.0 1.9 fusion.9
  211.9 3.2 fusion.4
  215.1 0.0 all-reduce.7.cloned.1.call-start
  215.2 99.4 %reduce-scatter.2.cloned.1.call-done = f32[8,2048]{1,0:T(8,128)} async-done(((f32[256,2048]{1,0:T(8,128)}), f32[8,2048]{1,0:T(8,128)}) %reduce-scatter.2.cloned.1.call-update) | async-done | bytes 65552 | tf_op jit(solution)/shard_map/reduce_scatter | solution.py:131
  314.6 0.0 all-gather.5.cloned.1.call-start
  314.6 125.9 %all-reduce.7.cloned.1.call-done = f32[8,2048]{1,0:T(8,128)} async-done(((f32[8,2048]{1,0:T(8,128)}), f32[8,2048]{1,0:T(8,128)}) %all-reduce.7.cloned.1.call-update) | async-done | bytes 65552 | tf_op jit(solution)/shard_map/psum | solution.py:132
  440.5 1.0 multiply_reduce_fusion
  441.5 1.5 multiply_convert_fusion
  443.1 0.0 all-reduce.9.cloned.1.call-start
  443.1 65.8 %all-gather.5.cloned.1.call-done = bf16[256,2048]{1,0:T(8,128)(2,1)} async-done(((bf16[8,2048]{1,0:T(8,128)(2,1)}), bf16[256,2048]{1,0:T(8,128)(2,1)}) %all-gather.5.cloned.1.call-update) | async-done | bytes 1048592 | tf_op jit(solution)/shard_map/all_gather | solution.py:134
  508.9 2.2 convolution_convert_fusion
  511.1 1.3 dynamic-slice
  513.1 132.5 %all-reduce.9.cloned.1.call-done = bf16[256,1664]{1,0:T(8,128)(2,1)} async-done(((bf16[256,1664]{1,0:T(8,128)(2,1)}), bf16[256,1664]{1,0:T(8,128)(2,1)}) %all-reduce.9.cloned.1.call-update) | async-done | bytes 851984
  645.6 0.7 dynamic-slice_convert_fusion
  646.4 0.1 constant_dynamic-slice_fusion
  646.4 2.3 collective-permute-start
  648.7 0.8 collective-permute-done
  649.5 0.1 add_bitcast_fusion
  649.6 0.6 copy.26
  (40 shorter events, 0.3 us)
Async XLA Ops:
  6.5 2.5 copy-start
  6.5 4.8 copy-start.9
  6.5 3.9 copy-start.5
  6.5 4.2 copy-start.11
  6.5 5.6 copy-start.3
  6.5 134.5 %all-reduce.5.cloned.1.call-start = ((), (), s32[]{:S(2)}) async-start(), calls=%async_computation.1 | async-start | bytes 131072 | tf_op jit(solution)/shard_map/psum | solution.py:112
  9.1 131.9 %copy-start.4 = (bf16[1,8,2048]{2,1,0:T(8,128)(2,1)S(1)}, bf16[1,8,2048]{2,1,0:T(8,128)(2,1)}, u32[]{:S(2)}) copy-start(bf16[1,8,2048]{2,1,0:T(8,128)(2,1)} %param.12) | copy-start | bytes 98308
  9.1 133.7 %copy-start.7 = (s32[2,128,8]{1,2,0:T(8,128)S(1)}, s32[2,128,8]{1,2,0:T(8,128)}, u32[]{:S(2)}) copy-start(s32[2,128,8]{1,2,0:T(8,128)} %param.18) | copy-start | bytes 24580
  10.3 132.6 %copy-start.8 = (f32[2,128,8]{1,2,0:T(8,128)S(1)}, f32[2,128,8]{1,2,0:T(8,128)}, u32[]{:S(2)}) copy-start(f32[2,128,8]{1,2,0:T(8,128)} %param.19) | copy-start | bytes 24580
  12.1 199.8 %copy-start.2 = (bf16[128,2048]{1,0:T(8,128)(2,1)S(1)}, bf16[128,2048]{1,0:T(8,128)(2,1)}, u32[]{:S(2)}) copy-start(bf16[128,2048]{1,0:T(8,128)(2,1)} %param.21) | copy-start | bytes 1572868
  13.0 197.0 %all-gather.3.cloned.1.call-start = ((), (), s32[]{:S(2)}) async-start(), calls=%async_computation.2 | async-start | bytes 1081344 | tf_op jit(solution)/shard_map/all_gather | solution.py:126
  142.7 171.9 %reduce-scatter.2.cloned.1.call-start = ((), (), s32[]{:S(2)}) async-start(), calls=%async_computation.3 | async-start | bytes 2162688 | tf_op jit(solution)/shard_map/reduce_scatter | solution.py:131
  210.0 1.9 copy-start.1
  215.1 293.8 %copy-start.6 = (bf16[64,1664]{1,0:T(8,128)(2,1)S(1)}, bf16[64,1664]{1,0:T(8,128)(2,1)}, u32[]{:S(2)}) copy-start(bf16[64,1664]{1,0:T(8,128)(2,1)} %param.22) | copy-start | bytes 638980
  215.1 434.4 %copy-start.10 = (f32[8]{0:T(128)S(1)}, f32[8]{0:T(128)}, u32[]{:S(2)}) copy-start(f32[8]{0:T(128)} %param.23) | copy-start | bytes 100
  215.1 225.4 %all-reduce.7.cloned.1.call-start = ((), (), s32[]{:S(2)}) async-start(), calls=%async_computation.4 | async-start | bytes 131072 | tf_op jit(solution)/shard_map/psum | solution.py:132
  314.6 194.3 %all-gather.5.cloned.1.call-start = ((), (), s32[]{:S(2)}) async-start(), calls=%async_computation.5 | async-start | bytes 1081344 | tf_op jit(solution)/shard_map/all_gather | solution.py:134
  443.1 202.6 %all-reduce.9.cloned.1.call-start = ((), (), s32[]{:S(2)}) async-start(), calls=%async_computation.6 | async-start | bytes 1703936
  646.4 3.1 collective-permute-start
Sparse Core Ops, SparseCore 0:
  13.1 127.8 all-reduce.4
  144.7 65.3 all-gather.2
  215.3 99.2 reduce-scatter.1
  316.9 123.6 all-reduce.6
  443.6 65.3 all-gather.4
  512.1 133.5 all-reduce.8
where the time goes:
time: 658 us; the launch traced here: 657 us
  waiting for transfers between devices  618 us (94%)
  between operations  14.4 us (2%)
  matrix products  9.92 us (2%)
  other arithmetic  9.7 us (1%)
    unnamed x7, waiting for transfers between devices  133 us
    psum x1, waiting for transfers between devices, body(): attention_out = lax.psum(partial_out, 'mp')  128 us
    psum x1, waiting for transfers between devices, body(): expert_total = lax.psum(expert_part, 'mp')  126 us
    reduce_scatter x1, waiting for transfers between devices, body(): lax.psum_scatter(expert_terms, ('guide', 'dp'), scatter_dimension=0, tile...  99.4 us
    all_gather x1, waiting for transfers between devices, body(): final_all = lax.all_gather(final, ('guide', 'dp'), axis=0, tiled=True)  65.8 us
    all_gather x1, waiting for transfers between devices, body(): piece = lax.all_gather(moe_in, ('guide', 'dp'), axis=0, tiled=True)  65.6 us
  transfers between devices with their start and end apart: 7, of which 7 were waited for; matrix products, arithmetic and copies ran while one was open for 0% of the time, Pallas kernels for 0%

commit v1 on v0

--- a/solution.py
+++ b/solution.py
@@ -123,7 +123,10 @@
         ),
         axis=1,
     )
-    piece = lax.all_gather(moe_in, ("guide", "dp"), axis=0, tiled=True)
+    piece = jnp.concatenate(
+        lax.all_to_all(jnp.stack([moe_in] * lax.axis_size(("guide", "dp"))), ("guide", "dp"), 0, 0),
+        axis=0,
+    )
     gate = jnp.dot(piece, expert_in[0], preferred_element_type=jnp.float32)
     upward = jnp.dot(piece, expert_in[1], preferred_element_type=jnp.float32)
     activated = (jax.nn.silu(gate) * upward * coefficient).astype(jnp.bfloat16)

time: 658 us -> 620 us (0.942)
  waiting for transfers between devices: 618 us -> 561 us
  starting transfers between devices: 2.5 us -> 21 us
    all_gather x1 -> x0, waiting for transfers between devices: 65.6 us -> none  [body(): piece = lax.all_gather(moe_in, ('guide', 'dp'), axis=0, tiled=True)]
    all_to_all x0 -> x1, starting transfers between devices: none -> 18.6 us  [body(): lax.all_to_all(jnp.stack([moe_in] * lax.axis_size(('guide', 'dp'))), ('gu...]
    all_to_all x0 -> x1, waiting for transfers between devices: none -> 14.8 us  [body(): lax.all_to_all(jnp.stack([moe_in] * lax.axis_size(('guide', 'dp'))), ('gu...]
    unnamed x7 -> x6, waiting for transfers between devices: 133 us -> 133 us
where the time goes in v1:
time: 620 us; the launch traced here: 619 us
  waiting for transfers between devices  561 us (90%)
  starting transfers between devices  21 us (3%)
  between operations  14 us (2%)
  matrix products  9.53 us (2%)
  other arithmetic  9.1 us (1%)
    unnamed x6, waiting for transfers between devices  133 us
    psum x1, waiting for transfers between devices, body(): attention_out = lax.psum(partial_out, 'mp')  128 us
    psum x1, waiting for transfers between devices, body(): expert_total = lax.psum(expert_part, 'mp')  126 us
    reduce_scatter x1, waiting for transfers between devices, body(): lax.psum_scatter(expert_terms, ('guide', 'dp'), scatter_dimension=0, tile...  93 us
    all_gather x1, waiting for transfers between devices, body(): final_all = lax.all_gather(final, ('guide', 'dp'), axis=0, tiled=True)  65.8 us
    all_to_all x1, starting transfers between devices, body(): lax.all_to_all(jnp.stack([moe_in] * lax.axis_size(('guide', 'dp'))), ('gu...  18.6 us
    all_to_all x1, waiting for transfers between devices, body(): lax.all_to_all(jnp.stack([moe_in] * lax.axis_size(('guide', 'dp'))), ('gu...  14.8 us
  transfers between devices with their start and end apart: 7, of which 7 were waited for; matrix products, arithmetic and copies ran while one was open for 0% of the time, Pallas kernels for 0%

profile of v1, /device:TPU:1, one launch (start us, length us, event | category | flops | bytes accessed | tf_op | source)
XLA Modules:
  0.0 618.8 jit_solution(14211623639099731368)
XLA Ops:
  6.5 0.0 all-reduce.5.cloned.1.call-start
  6.6 0.8 bitcast_convert_fusion
  7.4 0.8 broadcast_subtract_fusion
  8.2 0.9 fusion.26
  9.1 1.2 fusion
  10.3 0.1 fusion.70
  10.4 0.1 fusion.76
  10.5 0.2 fusion.10
  10.7 0.1 fusion.38
  10.9 0.1 copy.28
  10.9 0.2 fusion.60
  11.1 0.2 fusion.49
  11.4 0.2 fusion.40
  11.6 0.1 fusion.61
  11.7 0.2 fusion.9
  11.9 0.1 copy.33
  12.0 0.1 fusion.39
  12.1 0.9 fusion.14
  13.0 128.0 %all-reduce.5.cloned.1.call-done = f32[8,2048]{1,0:T(8,128)} async-done(((f32[8,2048]{1,0:T(8,128)}), f32[8,2048]{1,0:T(8,128)}) %all-reduce.5.cloned.1.call-update) | async-done | bytes 65552 | tf_op jit(solution)/shard_map/psum | solution.py:112
  141.0 1.0 fusion.29
  142.0 0.6 copy-done.3
  142.6 0.1 fusion.30
  142.7 1.1 stack.2
  143.8 18.6 %all-to-all-start = ((bf16[32,8,2048]{2,1,0:T(8,128)(2,1)}), bf16[32,8,2048]{2,1,0:T(8,128)(2,1)S(1)}, u32[]{:S(2)}, u32[]{:S(2)}) async-start(bf16[32,8,2048]{2,1,0:T(8,128)(2,1)} %stack.2), calls=%async_computation | async-start | bytes 2097152 | tf_op jit(solution)/shard_map/all_to_all | solution.py:127
  162.4 0.0 reduce-scatter.2.cloned.1.call-start
  162.4 0.1 copy.24
  162.6 0.1 copy.25
  162.7 1.3 select_reduce_fusion
  164.1 14.8 %all-to-all-done = bf16[32,8,2048]{2,1,0:T(8,128)(2,1)S(1)} async-done(((bf16[32,8,2048]{2,1,0:T(8,128)(2,1)}), bf16[32,8,2048]{2,1,0:T(8,128)(2,1)S(1)}, u32[]{:S(2)}, u32[]{:S(2)}) %all-to-all-start) | async-done | bytes 1048608 | tf_op jit(solution)/shard_map/all_to_all | solution.py:127
  178.9 1.5 fusion.7
  180.4 3.2 fusion.4
  183.6 0.0 all-reduce.7.cloned.1.call-start
  183.6 93.0 %reduce-scatter.2.cloned.1.call-done = f32[8,2048]{1,0:T(8,128)} async-done(((f32[256,2048]{1,0:T(8,128)}), f32[8,2048]{1,0:T(8,128)}) %reduce-scatter.2.cloned.1.call-update) | async-done | bytes 65552 | tf_op jit(solution)/shard_map/reduce_scatter | solution.py:134
  276.6 0.0 all-gather.2.cloned.1.call-start
  276.7 125.9 %all-reduce.7.cloned.1.call-done = f32[8,2048]{1,0:T(8,128)} async-done(((f32[8,2048]{1,0:T(8,128)}), f32[8,2048]{1,0:T(8,128)}) %all-reduce.7.cloned.1.call-update) | async-done | bytes 65552 | tf_op jit(solution)/shard_map/psum | solution.py:135
  402.6 1.0 multiply_reduce_fusion
  403.6 1.5 multiply_convert_fusion
  405.1 0.0 all-reduce.9.cloned.1.call-start
  405.2 65.8 %all-gather.2.cloned.1.call-done = bf16[256,2048]{1,0:T(8,128)(2,1)} async-done(((bf16[8,2048]{1,0:T(8,128)(2,1)}), bf16[256,2048]{1,0:T(8,128)(2,1)}) %all-gather.2.cloned.1.call-update) | async-done | bytes 1048592 | tf_op jit(solution)/shard_map/all_gather | solution.py:137
  471.0 2.2 convolution_convert_fusion
  473.2 1.3 dynamic-slice
  475.1 132.5 %all-reduce.9.cloned.1.call-done = bf16[256,1664]{1,0:T(8,128)(2,1)} async-done(((bf16[256,1664]{1,0:T(8,128)(2,1)}), bf16[256,1664]{1,0:T(8,128)(2,1)}) %all-reduce.9.cloned.1.call-update) | async-done | bytes 851984
  607.7 0.7 dynamic-slice_convert_fusion
  608.4 0.1 constant_dynamic-slice_fusion
  608.5 2.3 collective-permute-start
  610.8 0.8 collective-permute-done
  611.6 0.1 add_bitcast_fusion
  611.7 0.6 copy.26
  (42 shorter events, 0.3 us)
Async XLA Ops:
  6.5 2.5 copy-start
  6.5 4.8 copy-start.10
  6.5 3.9 copy-start.6
  6.5 4.2 copy-start.12
  6.5 5.6 copy-start.2
  6.5 134.5 %all-reduce.5.cloned.1.call-start = ((), (), s32[]{:S(2)}) async-start(), calls=%async_computation.2 | async-start | bytes 131072 | tf_op jit(solution)/shard_map/psum | solution.py:112
  9.1 131.9 %copy-start.5 = (bf16[1,8,2048]{2,1,0:T(8,128)(2,1)S(1)}, bf16[1,8,2048]{2,1,0:T(8,128)(2,1)}, u32[]{:S(2)}) copy-start(bf16[1,8,2048]{2,1,0:T(8,128)(2,1)} %param.12) | copy-start | bytes 98308
  142.0 0.6 copy-start.3
  142.7 19.8 %copy-start.8 = (s32[2,128,8]{1,2,0:T(8,128)S(1)}, s32[2,128,8]{1,2,0:T(8,128)}, u32[]{:S(2)}) copy-start(s32[2,128,8]{1,2,0:T(8,128)} %param.18) | copy-start | bytes 24580
  142.7 19.9 %copy-start.9 = (f32[2,128,8]{1,2,0:T(8,128)S(1)}, f32[2,128,8]{1,2,0:T(8,128)}, u32[]{:S(2)}) copy-start(f32[2,128,8]{1,2,0:T(8,128)} %param.19) | copy-start | bytes 24580
  143.8 35.1 %all-to-all-start = ((bf16[32,8,2048]{2,1,0:T(8,128)(2,1)}), bf16[32,8,2048]{2,1,0:T(8,128)(2,1)S(1)}, u32[]{:S(2)}, u32[]{:S(2)}) async-start(bf16[32,8,2048]{2,1,0:T(8,128)(2,1)} %stack.2), calls=%async_computation | async-start | bytes 2097152 | tf_op jit(solution)/shard_map/all_to_all | solution.py:127
  162.4 18.0 %copy-start.1 = (bf16[128,2048]{1,0:T(8,128)(2,1)S(1)}, bf16[128,2048]{1,0:T(8,128)(2,1)}, u32[]{:S(2)}) copy-start(bf16[128,2048]{1,0:T(8,128)(2,1)} %param.21) | copy-start | bytes 1572868
  162.4 114.3 %reduce-scatter.2.cloned.1.call-start = ((), (), s32[]{:S(2)}) async-start(), calls=%async_computation.3 | async-start | bytes 2162688 | tf_op jit(solution)/shard_map/reduce_scatter | solution.py:134
  183.5 219.0 %copy-start.4 = (bf16[8,2048]{1,0:T(8,128)(2,1)S(1)}, bf16[8,2048]{1,0:T(8,128)(2,1)}, u32[]{:S(2)}) copy-start(bf16[8,2048]{1,0:T(8,128)(2,1)} %copy-done.3) | copy-start | bytes 98308
  183.5 287.4 %copy-start.7 = (bf16[64,1664]{1,0:T(8,128)(2,1)S(1)}, bf16[64,1664]{1,0:T(8,128)(2,1)}, u32[]{:S(2)}) copy-start(bf16[64,1664]{1,0:T(8,128)(2,1)} %param.22) | copy-start | bytes 638980
  183.6 428.0 %copy-start.11 = (f32[8]{0:T(128)S(1)}, f32[8]{0:T(128)}, u32[]{:S(2)}) copy-start(f32[8]{0:T(128)} %param.23) | copy-start | bytes 100
  183.6 219.0 %all-reduce.7.cloned.1.call-start = ((), (), s32[]{:S(2)}) async-start(), calls=%async_computation.4 | async-start | bytes 131072 | tf_op jit(solution)/shard_map/psum | solution.py:135
  276.6 194.3 %all-gather.2.cloned.1.call-start = ((), (), s32[]{:S(2)}) async-start(), calls=%async_computation.5 | async-start | bytes 1081344 | tf_op jit(solution)/shard_map/all_gather | solution.py:137
  405.1 202.6 %all-reduce.9.cloned.1.call-start = ((), (), s32[]{:S(2)}) async-start(), calls=%async_computation.6 | async-start | bytes 1703936
  608.5 3.1 collective-permute-start
Sparse Core Ops, SparseCore 0:
  13.1 127.8 all-reduce.4
  183.7 92.8 reduce-scatter.1
  279.1 123.4 all-reduce.6
  405.6 65.3 all-gather.1
  474.1 133.5 all-reduce.8
